TPU v7x, 128 devices: a whole 4x4x4 slice. The times are simulated.
128 devices in a mesh: section: 16 (over z_lo, y, core), tensor: 8 (over x, z_hi).
Axes of the slice: x: 4, y: 4, z: 4 (z_hi: 2, z_lo: 2; z = z_hi * 2 + z_lo), core: 2. Of those that a mesh axis runs over, the one named last changes fastest.
Arguments:
- inflow: bfloat16 [16, 512, 12288], P('section', 'tensor'), may hold values from -60 to 60
- fresh: bfloat16 [512, 12288], P('tensor'), may hold values from -60 to 60
- stash_held: bfloat16 [16, 512, 12288], P('section', 'tensor'), may hold values from -60 to 60
- grad_in: bfloat16 [16, 512, 12288], P('section', 'tensor'), may hold values from -6 to 6
- query_gain: float32 [16, 12288], P('section', 'tensor'), may hold values from -3 to 3
- key_gain: float32 [16, 12288], P('section', 'tensor'), may hold values from -3 to 3
- value_gain: float32 [16, 12288], P('section', 'tensor'), may hold values from -4 to 4
Outputs:
- first_out: bfloat16 [16, 512, 12288], P('section', 'tensor')
- second_out: bfloat16 [16, 512, 12288], P('section', 'tensor')
- evicted: bfloat16 [16, 512, 12288], P('section', 'tensor')
- grad_out: bfloat16 [16, 512, 12288], P('section', 'tensor')
All inputs are finite; a program needn't handle non-finite values.
Results may differ from a plain program's by a relative error of at most 0.0068.
Values may be sent and summed in bfloat16 or wider, within the bound.
No kernel may reach another device: no remote copies, remote signals or barrier semaphores. Data moves between devices by JAX's collectives and lax.ppermute only.
A program may use at most 128 MiB of HBM per device.

v0:
```python
import jax
import jax.numpy as jnp
from jax import lax
from jax.sharding import PartitionSpec as P

HDIM = 128
epsilon = 1e-05
masked_score = -1e30


def from_partner(value, axis, distance):
    mask = 2**distance
    pairs = [(source, source ^ mask) for source in range(lax.axis_size(axis))]
    return lax.ppermute(value, axis, pairs)


def from_behind(x, axis, by):
    peers = lax.axis_size(axis)
    pairs = [(i, i + by) for i in range(peers) if 0 <= i + by < peers]
    return lax.ppermute(x, axis, pairs)


def normalize(tokens_in):
    values = tokens_in.astype(jnp.float32)
    factor = lax.rsqrt(jnp.mean(values * values, axis=-1, keepdims=True) + epsilon)
    return (values * factor, factor)


def heads_of(normed, feature_gain):
    scaled = (normed.astype(jnp.float32) * feature_gain).astype(jnp.bfloat16)
    return scaled.reshape(scaled.shape[0], -1, HDIM)


def softmax_causal(queries, key_heads):
    scores = jnp.einsum("ihd,jhd->hij", queries, key_heads, preferred_element_type=jnp.float32)
    scores = scores * HDIM ** (-0.5)
    length = queries.shape[0]
    row_index = lax.broadcasted_iota(jnp.int32, (length, length), 0)
    col_index = lax.broadcasted_iota(jnp.int32, (length, length), 1)
    scores = jnp.where(row_index >= col_index, scores, masked_score)
    largest = jnp.max(scores, axis=-1, keepdims=True)
    weights = jnp.exp(scores - largest)
    return weights / jnp.sum(weights, axis=-1, keepdims=True)


def forward(tokens_in, query_gain, key_gain, value_gain):
    scaled, factor = normalize(tokens_in)
    normed = scaled.astype(jnp.bfloat16)
    spread = lax.all_to_all(normed, "tensor", split_axis=1, concat_axis=0, tiled=True)
    queries = heads_of(spread, query_gain)
    key_heads = heads_of(spread, key_gain)
    value_heads = heads_of(spread, value_gain)
    weights = softmax_causal(queries, key_heads).astype(jnp.bfloat16)
    mixed_out = jnp.einsum("hij,jhd->ihd", weights, value_heads, preferred_element_type=jnp.float32)
    mixed_out = mixed_out.astype(jnp.bfloat16).reshape(spread.shape)
    merged = lax.all_to_all(mixed_out, "tensor", split_axis=0, concat_axis=1, tiled=True)
    return (tokens_in.astype(jnp.float32) + merged.astype(jnp.float32)).astype(jnp.bfloat16)


def backward(stash_rows, grad_rows, query_gain, key_gain, value_gain):
    scaled, factor = normalize(stash_rows)
    normed = scaled.astype(jnp.bfloat16)
    spread, grad_heads = (
        lax.all_to_all(normed, "tensor", split_axis=1, concat_axis=0, tiled=True),
        lax.all_to_all(grad_rows, "tensor", split_axis=1, concat_axis=0, tiled=True),
    )
    queries = heads_of(spread, query_gain)
    key_heads = heads_of(spread, key_gain)
    value_heads = heads_of(spread, value_gain)
    cotangent = grad_heads.reshape(grad_heads.shape[0], -1, HDIM)
    weights = softmax_causal(queries, key_heads)
    weights_low = weights.astype(jnp.bfloat16)
    value_grad = jnp.einsum(
        "hij,ihd->jhd", weights_low, cotangent, preferred_element_type=jnp.float32
    )
    prob_grad = jnp.einsum(
        "ihd,jhd->hij", cotangent, value_heads, preferred_element_type=jnp.float32
    )
    score_grad = weights * (prob_grad - jnp.sum(prob_grad * weights, axis=-1, keepdims=True))
    score_low = score_grad.astype(jnp.bfloat16)
    query_grad = jnp.einsum(
        "hij,jhd->ihd", score_low, key_heads, preferred_element_type=jnp.float32
    )
    key_grad = jnp.einsum("hij,ihd->jhd", score_low, queries, preferred_element_type=jnp.float32)
    query_grad = query_grad * HDIM ** (-0.5)
    key_grad = key_grad * HDIM ** (-0.5)
    head_shape = spread.shape
    normed_grad = (
        query_grad.reshape(head_shape) * query_gain + key_grad.reshape(head_shape) * key_gain
    )
    normed_grad = (normed_grad + value_grad.reshape(head_shape) * value_gain).astype(jnp.bfloat16)
    returned = lax.all_to_all(
        normed_grad, "tensor", split_axis=0, concat_axis=1, tiled=True
    ).astype(jnp.float32)
    inner = jnp.mean(returned * scaled, axis=-1, keepdims=True)
    return (grad_rows.astype(jnp.float32) + factor * (returned - scaled * inner)).astype(
        jnp.bfloat16
    )


def bit_order(count):
    numbers = list(range(count))
    return numbers


def evict_chain(payload, numbers):
    for bit_number in numbers:
        payload = from_partner(payload, "section", bit_number)
    return payload


def reload_chain(payload, numbers):
    for bit_number in numbers:
        payload = from_partner(payload, "section", bit_number)
    return payload


def per_device(inflow, fresh, stash_held, grad_in, query_gain, key_gain, value_gain):
    numbers = bit_order(lax.axis_size("section").bit_length() - 1)
    gain_query = query_gain[0]
    gain_key = key_gain[0]
    gain_value = value_gain[0]
    first_out = forward(inflow[0], gain_query, gain_key, gain_value)
    moved = from_behind(first_out, "section", 1)
    second_in = jnp.where(lax.axis_index("section") == 0, fresh, moved)
    second_out = forward(second_in, gain_query, gain_key, gain_value)
    evicted = evict_chain(inflow[0], numbers)
    stash_rows = reload_chain(stash_held[0], numbers)
    grad_out = backward(stash_rows, grad_in[0], gain_query, gain_key, gain_value)
    return (first_out[None], second_out[None], evicted[None], grad_out[None])


def solution(mesh):
    placed = (
        P("section", "tensor", None),
        P("tensor", None),
        P("section", "tensor", None),
        P("section", "tensor", None),
        P("section", "tensor"),
        P("section", "tensor"),
        P("section", "tensor"),
    )
    return jax.shard_map(
        per_device,
        mesh=mesh,
        in_specs=placed,
        out_specs=(
            P("section", "tensor", None),
            P("section", "tensor", None),
            P("section", "tensor", None),
            P("section", "tensor", None),
        ),
        check_vma=False,
    )
```

profile of v0, /device:TPU:0, one launch (start us, length us, event | category | flops | bytes accessed | tf_op | source)
XLA Modules:
  0.0 462.2 jit_solution(15312056894646589805)
XLA Ops:
  6.0 34.7 %collective-permute-done.6 = bf16[64,12288]{1,0:T(8,128)(2,1)S(1)} collective-permute-done((bf16[64,12288]{1,0:T(8,128)(2,1)S(1)}, bf16[64,12288]{1,0:T(8,128)(2,1)S(1)}, u32[]{:S(2)}, u32[]{:S(2)}) %collective-permute-start.6) | collective-permute-done | bytes 1572896 | tf_op jit(solution)/shard_map/ppermute | solution.py:14
  44.8 34.9 %collective-permute-done.7 = bf16[64,12288]{1,0:T(8,128)(2,1)} collective-permute-done((bf16[64,12288]{1,0:T(8,128)(2,1)S(1)}, bf16[64,12288]{1,0:T(8,128)(2,1)}, u32[]{:S(2)}, u32[]{:S(2)}) %collective-permute-start.7) | collective-permute-done | bytes 1572896 | tf_op jit(solution)/shard_map/ppermute | solution.py:14
  85.2 7.3 %all-to-all-start.5 = ((bf16[64,8,1536]{2,0,1:T(8,128)(2,1)}), bf16[64,8,1536]{2,0,1:T(8,128)(2,1)}, u32[]{:S(2)}, u32[]{:S(2)}) async-start(bf16[64,8,1536]{2,0,1:T(8,128)(2,1)} %copy.73), calls=%async_computation.5 | async-start | bytes 3145728 | tf_op jit(solution)/shard_map/all_to_all | solution.py:65
  96.4 15.8 %collective-permute-done.2 = bf16[64,12288]{1,0:T(8,128)(2,1)} collective-permute-done((bf16[64,12288]{1,0:T(8,128)(2,1)}, bf16[64,12288]{1,0:T(8,128)(2,1)}, u32[]{:S(2)}, u32[]{:S(2)}) %collective-permute-start.2) | collective-permute-done | bytes 1572896 | tf_op jit(solution)/shard_map/ppermute | solution.py:14
  114.0 14.0 %collective-permute-done.8 = bf16[64,12288]{1,0:T(8,128)(2,1)S(1)} collective-permute-done((bf16[64,12288]{1,0:T(8,128)(2,1)}, bf16[64,12288]{1,0:T(8,128)(2,1)S(1)}, u32[]{:S(2)}, u32[]{:S(2)}) %collective-permute-start.8) | collective-permute-done | bytes 1572896 | tf_op jit(solution)/shard_map/ppermute | solution.py:14
  128.3 5.1 %all-to-all-done.5 = bf16[64,8,1536]{2,0,1:T(8,128)(2,1)} async-done(((bf16[64,8,1536]{2,0,1:T(8,128)(2,1)}), bf16[64,8,1536]{2,0,1:T(8,128)(2,1)}, u32[]{:S(2)}, u32[]{:S(2)}) %all-to-all-start.5) | async-done | bytes 1572896 | tf_op jit(solution)/shard_map/all_to_all | solution.py:65
  139.4 17.0 %all-to-all-done = bf16[64,8,1536]{2,0,1:T(8,128)(2,1)} async-done(((bf16[64,8,1536]{2,0,1:T(8,128)(2,1)}), bf16[64,8,1536]{2,0,1:T(8,128)(2,1)}, u32[]{:S(2)}, u32[]{:S(2)}) %all-to-all-start) | async-done | bytes 1572896 | tf_op jit(solution)/shard_map/all_to_all | solution.py:49
  168.2 4.6 %reshape.202 = f32[512,12,128]{2,1,0:T(8,128)} reshape(f32[8,64,1536]{2,1,0:T(8,128)} %convert_bitcast_fusion.6) | data formatting | bytes 6291456 | tf_op jit(solution)/shard_map/convert_element_type | solution.py:30
  173.0 8.9 %all-to-all-done.4 = bf16[64,8,1536]{2,0,1:T(8,128)(2,1)S(1)} async-done(((bf16[64,8,1536]{2,0,1:T(8,128)(2,1)}), bf16[64,8,1536]{2,0,1:T(8,128)(2,1)S(1)}, u32[]{:S(2)}, u32[]{:S(2)}) %all-to-all-start.4) | async-done | bytes 1572896 | tf_op jit(solution)/shard_map/all_to_all | solution.py:64
  184.0 4.6 %reshape.208 = f32[512,12,128]{2,1,0:T(8,128)} reshape(f32[8,64,1536]{2,1,0:T(8,128)} %convert_bitcast_fusion.3) | data formatting | bytes 6291456 | tf_op jit(solution)/shard_map/convert_element_type | solution.py:30
  188.6 7.1 %multiply_convert_fusion.8 = (bf16[512,12,128]{2,1,0:T(8,128)(2,1)}, bf16[512,12,128]{2,1,0:T(8,128)(2,1)}, bf16[512,12,128]{2,1,0:T(8,128)(2,1)}, bf16[512,12,1...) fusion(f32[512,12,128]{2,1,0:T(8,128)} %reshape.202, f32[12,128]{1,0:T(8,128)S(1)} %bitcast.93, ...), kind=kLoop, calls=%fused_computation.44 | loop fusion | flops 9437184 | bytes 15747072 | tf_op jit(solution)/shard_map/convert_element_type | solution.py:30
  207.3 8.2 %fusion.70 = (f32[12,512]{1,0:T(8,128)S(1)}, f32[12,512,512]{1,2,0:T(8,128)}) fusion(f32[12,512,512]{1,2,0:T(8,128)S(1)} %fusion.51, pred[512,512]{0,1:T(8,128)(4,1)S(1)} %iota_compare_fusion), kind=kOutput, calls=%fused_computation.110 | output fusion | flops 18874880 | bytes 25452544 | tf_op jit(solution)/shard_map/sub | solution.py:42
  215.5 7.9 %fusion.54 = bf16[512,12,128]{0,2,1:T(8,128)(2,1)} fusion(f32[12,512,512]{1,2,0:T(8,128)} %get-tuple-element.21, f32[12,512]{1,0:T(8,128)S(1)} %get-tuple-element.20, bf16[512,12,128]{2,1,0:T(8,128)(2,1)} %get-tuple-element.12), kind=kOutput, calls=%fused_computation.94 | convolution fusion | flops 812384256 | bytes 15753216 | tf_op jit(solution)/shard_map/hij,jhd->ihd/dot_general | solution.py:54
  231.8 4.5 all-to-all-start.1
  236.3 10.6 %fusion.72 = (f32[12,512]{1,0:T(8,128)S(1)}, f32[12,512,512]{1,2,0:T(8,128)}) fusion(pred[512,512]{0,1:T(8,128)(4,1)S(1)} %iota_compare_fusion, bf16[512,12,128]{0,2,1:T(8,128)(2,1)} %copy.79, bf16[512,12,128]{0,2,1:T(8,128)(2,1)S(1)} %copy.76), kind=kOutput, calls=%fused_computation.112 | convolution fusion | flops 817889792 | bytes 16015360 | tf_op jit(solution)/shard_map/sub | solution.py:42
  246.9 8.8 %fusion.37 = f32[512,12,128]{2,0,1:T(8,128)} fusion(bf16[512,12,128]{2,1,0:T(8,128)(2,1)} %reshape.197, f32[12,512,512]{1,2,0:T(8,128)} %get-tuple-element.25, f32[12,512]{1,0:T(8,128)S(1)} %get-tuple-element.24), kind=kOutput, calls=%fused_computation.76 | convolution fusion | flops 811597824 | bytes 17326080 | tf_op jit(solution)/shard_map/hij,ihd->jhd/dot_general | solution.py:73
  256.8 9.5 %fusion.3 = (f32[12,512]{1,0:T(8,128)S(1)}, f32[12,512,512]{2,1,0:T(8,128)}) fusion(f32[12,512,512]{1,2,0:T(8,128)S(1)} %copy-done.8, f32[12,512]{1,0:T(8,128)S(1)} %get-tuple-element.24, bf16[512,12,128]{2,1,0:T(8,128)(2,1)} %reshape.197, bf16[512,12,128]{2,1,0:T(8,128)(2,1)} %get-tuple-element.19), kind=kOutput, calls=%fused_computation.5 | convolution fusion | flops 814737408 | bytes 28360704 | tf_op jit(solution)/shard_map/ihd,jhd->hij/dot_general | solution.py:76
  266.3 7.2 %fusion.5 = bf16[12,512,512]{1,2,0:T(8,128)(2,1)S(1)} fusion(f32[12,512,512]{2,1,0:T(8,128)} %get-tuple-element.27, f32[12,512]{1,0:T(8,128)S(1)} %get-tuple-element.26, f32[12,512,512]{1,2,0:T(8,128)S(1)} %copy-done.8, f32[12,512]{1,0:T(8,128)S(1)} %get-tuple-element.24), kind=kLoop, calls=%fused_computation.7 | loop fusion | flops 12582912 | bytes 31506432 | tf_op jit(solution)/shard_map/convert_element_type | solution.py:80
  281.6 4.7 %reshape.200 = f32[8,64,1536]{2,1,0:T(8,128)} reshape(f32[512,12,128]{2,1,0:T(8,128)} %copy.83) | data formatting | bytes 6291456 | tf_op jit(solution)/shard_map/reshape | solution.py:91
  286.3 5.1 %copy.78 = f32[512,12,128]{2,1,0:T(8,128)} copy(f32[512,12,128]{0,2,1:T(8,128)} %multiply_bitcast_fusion.1) | data formatting | bytes 6291456 | tf_op jit(solution)/shard_map/mul | solution.py:85
  291.4 4.8 %reshape.198 = f32[8,64,1536]{2,1,0:T(8,128)} reshape(f32[512,12,128]{2,1,0:T(8,128)} %copy.78) | data formatting | bytes 6291456 | tf_op jit(solution)/shard_map/reshape | solution.py:89
  296.2 6.6 %multiply_bitcast_fusion = f32[512,12,128]{0,2,1:T(8,128)} fusion(bf16[512,12,128]{0,2,1:T(8,128)(2,1)S(1)} %copy-done.9, bf16[12,512,512]{1,2,0:T(8,128)(2,1)} %copy-done), kind=kOutput, calls=%fused_computation.73 | convolution fusion | flops 806092800 | bytes 11010048 | tf_op jit(solution)/shard_map/hij,ihd->jhd/dot_general | solution.py:84
  302.8 5.1 %copy.81 = f32[512,12,128]{2,1,0:T(8,128)} copy(f32[512,12,128]{0,2,1:T(8,128)} %multiply_bitcast_fusion) | data formatting | bytes 6291456 | tf_op jit(solution)/shard_map/mul | solution.py:86
  307.9 4.7 %reshape.199 = f32[8,64,1536]{2,1,0:T(8,128)} reshape(f32[512,12,128]{2,1,0:T(8,128)} %copy.81) | data formatting | bytes 6291456 | tf_op jit(solution)/shard_map/reshape | solution.py:89
  312.6 6.1 %add_convert_fusion = bf16[8,64,1536]{2,1,0:T(8,128)(2,1)} fusion(f32[8,64,1536]{2,1,0:T(8,128)} %reshape.200, f32[8,64,1536]{2,1,0:T(8,128)} %reshape.199, f32[8,64,1536]{2,1,0:T(8,128)} %reshape.198, f32[1536]{0:T(1024)S(1)} %reduce, f32[1536]{0:T(1024)S(1)} %reduce.2, f32[1536]{0:T(1024)S(1)} %reduce.1), kind=kLoop, calls=%fused_computation.72 | loop fusion | flops 4718592 | bytes 11028480 | tf_op jit(solution)/shard_map/convert_element_type | solution.py:91
  318.7 7.2 %all-to-all-start.6 = ((bf16[8,64,1536]{2,1,0:T(8,128)(2,1)}), bf16[8,64,1536]{2,1,0:T(8,128)(2,1)S(1)}, u32[]{:S(2)}, u32[]{:S(2)}) async-start(bf16[8,64,1536]{2,1,0:T(8,128)(2,1)} %add_convert_fusion), calls=%async_computation.6 | async-start | bytes 3145728 | tf_op jit(solution)/shard_map/all_to_all | solution.py:92
  333.6 28.7 %all-to-all-done.6 = bf16[8,64,1536]{2,1,0:T(8,128)(2,1)S(1)} async-done(((bf16[8,64,1536]{2,1,0:T(8,128)(2,1)}), bf16[8,64,1536]{2,1,0:T(8,128)(2,1)S(1)}, u32[]{:S(2)}, u32[]{:S(2)}) %all-to-all-start.6) | async-done | bytes 1572896 | tf_op jit(solution)/shard_map/all_to_all | solution.py:92
  379.5 17.8 %all-to-all-done.2 = bf16[64,8,1536]{2,0,1:T(8,128)(2,1)} async-done(((bf16[64,8,1536]{2,0,1:T(8,128)(2,1)}), bf16[64,8,1536]{2,0,1:T(8,128)(2,1)}, u32[]{:S(2)}, u32[]{:S(2)}) %all-to-all-start.2) | async-done | bytes 1572896 | tf_op jit(solution)/shard_map/all_to_all | solution.py:49
  406.4 8.2 %fusion.71 = (f32[12,512]{1,0:T(8,128)S(1)}, f32[12,512,512]{1,2,0:T(8,128)}) fusion(f32[12,512,512]{1,2,0:T(8,128)S(1)} %fusion.47, pred[512,512]{0,1:T(8,128)(4,1)S(1)} %iota_compare_fusion), kind=kOutput, calls=%fused_computation.111 | output fusion | flops 18874880 | bytes 25452544 | tf_op jit(solution)/shard_map/sub | solution.py:42
  414.6 6.1 %fusion.57 = bf16[512,12,128]{0,2,1:T(8,128)(2,1)S(1)} fusion(f32[12,512,512]{1,2,0:T(8,128)} %get-tuple-element.23, f32[12,512]{1,0:T(8,128)S(1)} %get-tuple-element.22, bf16[512,12,128]{2,1,0:T(8,128)(2,1)S(1)} %get-tuple-element.9), kind=kOutput, calls=%fused_computation.95 | convolution fusion | flops 812384256 | bytes 15753216 | tf_op jit(solution)/shard_map/hij,jhd->ihd/dot_general | solution.py:54
  427.8 4.5 all-to-all-start.3
  435.6 20.6 %all-to-all-done.3 = bf16[8,64,1536]{2,1,0:T(8,128)(2,1)S(1)} async-done(((bf16[8,64,1536]{2,1,0:T(8,128)(2,1)}), bf16[8,64,1536]{2,1,0:T(8,128)(2,1)S(1)}, u32[]{:S(2)}, u32[]{:S(2)}) %all-to-all-start.3) | async-done | bytes 1572896 | tf_op jit(solution)/shard_map/all_to_all | solution.py:56
  (97 shorter events, 120.2 us)
Async XLA Ops:
  0.6 3.7 collective-permute-start.5
  4.3 36.4 %collective-permute-start.6 = (bf16[64,12288]{1,0:T(8,128)(2,1)S(1)}, bf16[64,12288]{1,0:T(8,128)(2,1)S(1)}, u32[]{:S(2)}, u32[]{:S(2)}) collective-permute-start(bf16[64,12288]{1,0:T(8,128)(2,1)S(1)} %collective-permute-done.5), channel_id=1, source_target_pairs={{0,16},{8,24},{16,0},{24,8},{32,48},{40,56},{48,32},{56,40},{64,80... | collective-permute-start | bytes 4718600 | tf_op jit(solution)/shard_map/ppermute | solution.py:14
  6.0 38.1 %collective-permute-start.1 = (bf16[64,12288]{1,0:T(8,128)(2,1)}, bf16[64,12288]{1,0:T(8,128)(2,1)}, u32[]{:S(2)}, u32[]{:S(2)}) collective-permute-start(bf16[64,12288]{1,0:T(8,128)(2,1)} %bitcast.79), channel_id=1, source_target_pairs={{0,8},{8,0},{16,24},{24,16},{32,40},{40,32},{48,56},{56,48},{64,72... | collective-permute-start | bytes 4718600 | tf_op jit(solution)/shard_map/ppermute | solution.py:14
  40.8 38.9 %collective-permute-start.7 = (bf16[64,12288]{1,0:T(8,128)(2,1)S(1)}, bf16[64,12288]{1,0:T(8,128)(2,1)}, u32[]{:S(2)}, u32[]{:S(2)}) collective-permute-start(bf16[64,12288]{1,0:T(8,128)(2,1)S(1)} %collective-permute-done.6), channel_id=1, source_target_pairs={{0,32},{8,40},{16,48},{24,56},{32,0},{40,8},{48,16},{56,24},{64,96... | collective-permute-start | bytes 4718600 | tf_op jit(solution)/shard_map/ppermute | solution.py:14
  44.1 68.0 %collective-permute-start.2 = (bf16[64,12288]{1,0:T(8,128)(2,1)}, bf16[64,12288]{1,0:T(8,128)(2,1)}, u32[]{:S(2)}, u32[]{:S(2)}) collective-permute-start(bf16[64,12288]{1,0:T(8,128)(2,1)} %collective-permute-done.1), channel_id=1, source_target_pairs={{0,16},{8,24},{16,0},{24,8},{32,48},{40,56},{48,32},{56,40},{64,80... | collective-permute-start | bytes 4718600 | tf_op jit(solution)/shard_map/ppermute | solution.py:14
  79.6 48.3 %collective-permute-start.8 = (bf16[64,12288]{1,0:T(8,128)(2,1)}, bf16[64,12288]{1,0:T(8,128)(2,1)S(1)}, u32[]{:S(2)}, u32[]{:S(2)}) collective-permute-start(bf16[64,12288]{1,0:T(8,128)(2,1)} %collective-permute-done.7), channel_id=1, source_target_pairs={{0,64},{8,72},{16,80},{24,88},{32,96},{40,104},{48,112},{56,120},{... | collective-permute-start | bytes 4718600 | tf_op jit(solution)/shard_map/ppermute | solution.py:14
  83.6 8.9 %copy-start.3 = (bf16[1,64,12288]{2,1,0:T(8,128)(2,1)S(1)}, bf16[1,64,12288]{2,1,0:T(8,128)(2,1)}, u32[]{:S(2)}) copy-start(bf16[1,64,12288]{2,1,0:T(8,128)(2,1)} %param.7) | copy-start | bytes 4718596
  85.2 48.2 %all-to-all-start.5 = ((bf16[64,8,1536]{2,0,1:T(8,128)(2,1)}), bf16[64,8,1536]{2,0,1:T(8,128)(2,1)}, u32[]{:S(2)}, u32[]{:S(2)}) async-start(bf16[64,8,1536]{2,0,1:T(8,128)(2,1)} %copy.73), calls=%async_computation.5 | async-start | bytes 3145728 | tf_op jit(solution)/shard_map/all_to_all | solution.py:65
  112.1 60.7 %collective-permute-start.3 = (bf16[64,12288]{1,0:T(8,128)(2,1)}, bf16[64,12288]{1,0:T(8,128)(2,1)}, u32[]{:S(2)}, u32[]{:S(2)}) collective-permute-start(bf16[64,12288]{1,0:T(8,128)(2,1)} %collective-permute-done.2), channel_id=1, source_target_pairs={{0,32},{8,40},{16,48},{24,56},{32,0},{40,8},{48,16},{56,24},{64,96... | collective-permute-start | bytes 4718600 | tf_op jit(solution)/shard_map/ppermute | solution.py:14
  127.9 10.2 %copy-start.1 = (bf16[64,12288]{1,0:T(8,128)(2,1)}, bf16[64,12288]{1,0:T(8,128)(2,1)S(1)}, u32[]{:S(2)}) copy-start(bf16[64,12288]{1,0:T(8,128)(2,1)S(1)} %collective-permute-done.8) | copy-start | bytes 4718596
  133.4 22.9 %all-to-all-start = ((bf16[64,8,1536]{2,0,1:T(8,128)(2,1)}), bf16[64,8,1536]{2,0,1:T(8,128)(2,1)}, u32[]{:S(2)}, u32[]{:S(2)}) async-start(bf16[64,8,1536]{2,0,1:T(8,128)(2,1)} %fusion.36), calls=%async_computation | async-start | bytes 3145728 | tf_op jit(solution)/shard_map/all_to_all | solution.py:49
  138.1 22.4 %copy-start.12 = (f32[1,1536]{1,0:T(1,128)S(1)}, f32[1,1536]{1,0:T(1,128)}, u32[]{:S(2)}) copy-start(f32[1,1536]{1,0:T(1,128)} %param.11) | copy-start | bytes 18436
  138.1 22.4 %copy-start.13 = (f32[1,1536]{1,0:T(1,128)S(1)}, f32[1,1536]{1,0:T(1,128)}, u32[]{:S(2)}) copy-start(f32[1,1536]{1,0:T(1,128)} %param.12) | copy-start | bytes 18436
  138.1 22.4 %copy-start.14 = (f32[1,1536]{1,0:T(1,128)S(1)}, f32[1,1536]{1,0:T(1,128)}, u32[]{:S(2)}) copy-start(f32[1,1536]{1,0:T(1,128)} %param.13) | copy-start | bytes 18436
  156.4 25.5 %all-to-all-start.4 = ((bf16[64,8,1536]{2,0,1:T(8,128)(2,1)}), bf16[64,8,1536]{2,0,1:T(8,128)(2,1)S(1)}, u32[]{:S(2)}, u32[]{:S(2)}) async-start(bf16[64,8,1536]{2,0,1:T(8,128)(2,1)} %bitcast.75), calls=%async_computation.4 | async-start | bytes 3145728 | tf_op jit(solution)/shard_map/all_to_all | solution.py:64
  172.8 160.8 %collective-permute-start.4 = (bf16[64,12288]{1,0:T(8,128)(2,1)}, bf16[64,12288]{1,0:T(8,128)(2,1)}, u32[]{:S(2)}, u32[]{:S(2)}) collective-permute-start(bf16[64,12288]{1,0:T(8,128)(2,1)} %collective-permute-done.3), channel_id=1, source_target_pairs={{0,64},{8,72},{16,80},{24,88},{32,96},{40,104},{48,112},{56,120},{... | collective-permute-start | bytes 4718600 | tf_op jit(solution)/shard_map/ppermute | solution.py:14
  231.8 86.9 %all-to-all-start.1 = ((bf16[8,64,1536]{2,1,0:T(8,128)(2,1)}), bf16[8,64,1536]{2,1,0:T(8,128)(2,1)}, u32[]{:S(2)}, u32[]{:S(2)}) async-start(bf16[8,64,1536]{2,1,0:T(8,128)(2,1)} %all_to_all.34), calls=%async_computation.1 | async-start | bytes 3145728 | tf_op jit(solution)/shard_map/all_to_all | solution.py:56
  246.9 9.9 %copy-start.8 = (f32[12,512,512]{1,2,0:T(8,128)S(1)}, f32[12,512,512]{1,2,0:T(8,128)}, u32[]{:S(2)}) copy-start(f32[12,512,512]{1,2,0:T(8,128)} %get-tuple-element.25) | copy-start | bytes 37748740
  273.5 4.2 copy-start
  273.5 4.2 copy-start.10
  291.4 4.8 %copy-start.9 = (bf16[512,12,128]{0,2,1:T(8,128)(2,1)S(1)}, bf16[512,12,128]{0,2,1:T(8,128)(2,1)}, u32[]{:S(2)}) copy-start(bf16[512,12,128]{0,2,1:T(8,128)(2,1)} %copy.79) | copy-start | bytes 4718596
  318.7 43.6 %all-to-all-start.6 = ((bf16[8,64,1536]{2,1,0:T(8,128)(2,1)}), bf16[8,64,1536]{2,1,0:T(8,128)(2,1)S(1)}, u32[]{:S(2)}, u32[]{:S(2)}) async-start(bf16[8,64,1536]{2,1,0:T(8,128)(2,1)} %add_convert_fusion), calls=%async_computation.6 | async-start | bytes 3145728 | tf_op jit(solution)/shard_map/all_to_all | solution.py:92
  331.1 33.6 %collective-permute-start = (bf16[64,12288]{1,0:T(8,128)(2,1)}, bf16[64,12288]{1,0:T(8,128)(2,1)}, u32[]{:S(2)}, u32[]{:S(2)}) collective-permute-start(bf16[64,12288]{1,0:T(8,128)(2,1)} %fusion.26), channel_id=1, source_target_pairs={{0,8},{8,16},{16,24},{24,32},{32,40},{40,48},{48,56},{56,64},{64,7... | collective-permute-start | bytes 4718600 | tf_op jit(solution)/shard_map/ppermute | solution.py:20
  362.7 1.4 copy-start.2
  362.9 1.8 copy-start.11
  365.5 1.7 copy-start.5
  367.2 30.0 %all-to-all-start.2 = ((bf16[64,8,1536]{2,0,1:T(8,128)(2,1)}), bf16[64,8,1536]{2,0,1:T(8,128)(2,1)}, u32[]{:S(2)}, u32[]{:S(2)}) async-start(bf16[64,8,1536]{2,0,1:T(8,128)(2,1)} %bitcast.84), calls=%async_computation.2 | async-start | bytes 3145728 | tf_op jit(solution)/shard_map/all_to_all | solution.py:49
  371.7 4.0 copy-start.7
  423.7 8.6 %copy-start.4 = (bf16[1,64,12288]{2,1,0:T(8,128)(2,1)S(1)}, bf16[1,64,12288]{2,1,0:T(8,128)(2,1)}, u32[]{:S(2)}) copy-start(bf16[1,64,12288]{2,1,0:T(8,128)(2,1)} %param.7) | copy-start | bytes 4718596
  427.8 28.4 %all-to-all-start.3 = ((bf16[8,64,1536]{2,1,0:T(8,128)(2,1)}), bf16[8,64,1536]{2,1,0:T(8,128)(2,1)S(1)}, u32[]{:S(2)}, u32[]{:S(2)}) async-start(bf16[8,64,1536]{2,1,0:T(8,128)(2,1)} %all_to_all.73), calls=%async_computation.3 | async-start | bytes 3145728 | tf_op jit(solution)/shard_map/all_to_all | solution.py:56
  456.6 1.4 copy-start.6
where the time goes:
time: 470 us; the launch traced here: 462 us
  waiting for transfers between devices  201 us (43%)
  local copies, waits for them, and re-layouts  85.5 us (18%)
  other arithmetic  67.9 us (14%)
  matrix products  58.2 us (12%)
  starting transfers between devices  48.6 us (10%)
    ppermute x8, waiting for transfers between devices, from_partner(): return lax.ppermute(value, axis, pairs)  103 us
    all_to_all x2, waiting for transfers between devices, forward(): lax.all_to_all(normed, 'tensor', split_axis=1, concat_axis=0, tiled=True)  34.7 us
    all_to_all x1, waiting for transfers between devices, backward(): lax.all_to_all(normed_grad, 'tensor', split_axis=0, concat_axis=1, tiled=...  28.7 us
    all_to_all x2, waiting for transfers between devices, forward(): lax.all_to_all(mixed_out, 'tensor', split_axis=0, concat_axis=1, tiled=True)  20.6 us
    convert_element_type x5, local copies, waits for them, and re-layouts, heads_of(): scaled = (normed.astype(jnp.float32) * feature_gain).astype(jnp.bfloat16)  19 us
    convert_element_type x5, other arithmetic, heads_of(): scaled = (normed.astype(jnp.float32) * feature_gain).astype(jnp.bfloat16)  17.7 us
    sub x2, other arithmetic, softmax_causal(): weights = jnp.exp(scores - largest)  16.4 us
    dot_general x2, matrix products, forward(): jnp.einsum('hij,jhd->ihd', weights, value_heads, preferred_element_type=j...  14.1 us
  transfers between devices with their start and end apart: 16, of which 11 were waited for; matrix products, arithmetic and copies ran while one was open for 36% of the time, Pallas kernels for 0%

commit v1 on v0

--- a/solution.py
+++ b/solution.py
@@ -89,8 +89,11 @@
         query_grad.reshape(head_shape) * query_gain + key_grad.reshape(head_shape) * key_gain
     )
     normed_grad = (normed_grad + value_grad.reshape(head_shape) * value_gain).astype(jnp.bfloat16)
-    returned = lax.all_to_all(
-        normed_grad, "tensor", split_axis=0, concat_axis=1, tiled=True
+    returned = jnp.concatenate(
+        lax.all_to_all(
+            jnp.stack(jnp.split(normed_grad, lax.axis_size("tensor"), axis=0)), "tensor", 0, 0
+        ),
+        axis=1,
     ).astype(jnp.float32)
     inner = jnp.mean(returned * scaled, axis=-1, keepdims=True)
     return (grad_rows.astype(jnp.float32) + factor * (returned - scaled * inner)).astype(

time: 470 us -> 452 us (0.962)
  local copies, waits for them, and re-layouts: 85.5 us -> 77.5 us
    mul x2 -> x0, local copies, waits for them, and re-layouts: 10.2 us -> none  [the longest x1 5.1 us: backward(): key_grad = key_grad * HDIM ** (-0.5)]
    unnamed x33 -> x52, local copies, waits for them, and re-layouts: 9.98 us -> 14.7 us
  transfers between devices with their start and end apart: 16 -> 16, of which waited for: 11 -> 12; matrix products, arithmetic and copies ran while one was open for 36% -> 34% of each run, Pallas kernels for 0% -> 0%
where the time goes in v1:
time: 452 us; the launch traced here: 444 us
  waiting for transfers between devices  197 us (44%)
  local copies, waits for them, and re-layouts  77.5 us (17%)
  other arithmetic  66.7 us (15%)
  matrix products  54.5 us (12%)
  starting transfers between devices  47.3 us (10%)
    ppermute x8, waiting for transfers between devices, from_partner(): return lax.ppermute(value, axis, pairs)  103 us
    all_to_all x2, waiting for transfers between devices, forward(): lax.all_to_all(normed, 'tensor', split_axis=1, concat_axis=0, tiled=True)  34.7 us
    all_to_all x1, waiting for transfers between devices, backward(): lax.all_to_all(jnp.stack(jnp.split(normed_grad, lax.axis_size('tensor'),...  28.6 us
    all_to_all x2, waiting for transfers between devices, forward(): lax.all_to_all(mixed_out, 'tensor', split_axis=0, concat_axis=1, tiled=True)  21.2 us
    convert_element_type x5, local copies, waits for them, and re-layouts, heads_of(): scaled = (normed.astype(jnp.float32) * feature_gain).astype(jnp.bfloat16)  19.1 us
    convert_element_type x5, other arithmetic, heads_of(): scaled = (normed.astype(jnp.float32) * feature_gain).astype(jnp.bfloat16)  17.9 us
    sub x2, other arithmetic, softmax_causal(): weights = jnp.exp(scores - largest)  16.4 us
    unnamed x52, local copies, waits for them, and re-layouts  14.7 us
  transfers between devices with their start and end apart: 16, of which 12 were waited for; matrix products, arithmetic and copies ran while one was open for 34% of the time, Pallas kernels for 0%

profile of v1, /device:TPU:0, one launch (start us, length us, event | category | flops | bytes accessed | tf_op | source)
XLA Modules:
  0.0 444.3 jit_solution(747477331206184728)
XLA Ops:
  6.0 34.7 %collective-permute-done.6 = bf16[64,12288]{1,0:T(8,128)(2,1)S(1)} collective-permute-done((bf16[64,12288]{1,0:T(8,128)(2,1)S(1)}, bf16[64,12288]{1,0:T(8,128)(2,1)S(1)}, u32[]{:S(2)}, u32[]{:S(2)}) %collective-permute-start.6) | collective-permute-done | bytes 1572896 | tf_op jit(solution)/shard_map/ppermute | solution.py:14
  44.8 34.9 %collective-permute-done.7 = bf16[64,12288]{1,0:T(8,128)(2,1)} collective-permute-done((bf16[64,12288]{1,0:T(8,128)(2,1)S(1)}, bf16[64,12288]{1,0:T(8,128)(2,1)}, u32[]{:S(2)}, u32[]{:S(2)}) %collective-permute-start.7) | collective-permute-done | bytes 1572896 | tf_op jit(solution)/shard_map/ppermute | solution.py:14
  85.2 7.3 %all-to-all-start.5 = ((bf16[64,8,1536]{2,0,1:T(8,128)(2,1)}), bf16[64,8,1536]{2,0,1:T(8,128)(2,1)}, u32[]{:S(2)}, u32[]{:S(2)}) async-start(bf16[64,8,1536]{2,0,1:T(8,128)(2,1)} %copy.132), calls=%async_computation.5 | async-start | bytes 3145728 | tf_op jit(solution)/shard_map/all_to_all | solution.py:65
  96.4 15.8 %collective-permute-done.2 = bf16[64,12288]{1,0:T(8,128)(2,1)} collective-permute-done((bf16[64,12288]{1,0:T(8,128)(2,1)}, bf16[64,12288]{1,0:T(8,128)(2,1)}, u32[]{:S(2)}, u32[]{:S(2)}) %collective-permute-start.2) | collective-permute-done | bytes 1572896 | tf_op jit(solution)/shard_map/ppermute | solution.py:14
  114.0 14.0 %collective-permute-done.8 = bf16[64,12288]{1,0:T(8,128)(2,1)S(1)} collective-permute-done((bf16[64,12288]{1,0:T(8,128)(2,1)}, bf16[64,12288]{1,0:T(8,128)(2,1)S(1)}, u32[]{:S(2)}, u32[]{:S(2)}) %collective-permute-start.8) | collective-permute-done | bytes 1572896 | tf_op jit(solution)/shard_map/ppermute | solution.py:14
  128.3 5.1 %all-to-all-done.5 = bf16[64,8,1536]{2,0,1:T(8,128)(2,1)} async-done(((bf16[64,8,1536]{2,0,1:T(8,128)(2,1)}), bf16[64,8,1536]{2,0,1:T(8,128)(2,1)}, u32[]{:S(2)}, u32[]{:S(2)}) %all-to-all-start.5) | async-done | bytes 1572896 | tf_op jit(solution)/shard_map/all_to_all | solution.py:65
  133.4 4.3 all-to-all-start
  139.4 17.0 %all-to-all-done = bf16[64,8,1536]{2,0,1:T(8,128)(2,1)} async-done(((bf16[64,8,1536]{2,0,1:T(8,128)(2,1)}), bf16[64,8,1536]{2,0,1:T(8,128)(2,1)}, u32[]{:S(2)}, u32[]{:S(2)}) %all-to-all-start) | async-done | bytes 1572896 | tf_op jit(solution)/shard_map/all_to_all | solution.py:49
  156.4 4.1 all-to-all-start.4
  164.6 4.3 copy.142
  172.4 4.6 %reshape.183 = f32[512,12,128]{2,1,0:T(8,128)} reshape(f32[8,64,1536]{2,1,0:T(8,128)} %convert_bitcast_fusion.6) | data formatting | bytes 6291456 | tf_op jit(solution)/shard_map/convert_element_type | solution.py:30
  177.5 4.3 all-to-all-done.4
  184.0 4.7 %reshape.189 = f32[512,12,128]{2,1,0:T(8,128)} reshape(f32[8,64,1536]{2,1,0:T(8,128)} %convert_bitcast_fusion.3) | data formatting | bytes 6291456 | tf_op jit(solution)/shard_map/convert_element_type | solution.py:30
  188.6 7.3 %multiply_convert_fusion.8 = (bf16[512,12,128]{2,1,0:T(8,128)(2,1)}, bf16[512,12,128]{2,1,0:T(8,128)(2,1)}, bf16[512,12,128]{2,1,0:T(8,128)(2,1)}, bf16[512,12,1...) fusion(f32[512,12,128]{2,1,0:T(8,128)} %reshape.183, f32[12,128]{1,0:T(8,128)S(1)} %bitcast.135, ...), kind=kLoop, calls=%fused_computation.44 | loop fusion | flops 9437184 | bytes 15747072 | tf_op jit(solution)/shard_map/convert_element_type | solution.py:30
  199.2 4.3 copy.138
  203.4 10.5 %fusion.75 = (f32[12,512]{1,0:T(8,128)S(1)}, f32[12,512,512]{1,2,0:T(8,128)}) fusion(pred[512,512]{0,1:T(8,128)(4,1)S(1)} %iota_compare_fusion, bf16[512,12,128]{0,2,1:T(8,128)(2,1)} %copy.138, bf16[512,12,128]{0,2,1:T(8,128)(2,1)S(1)} %copy.135), kind=kOutput, calls=%fused_computation.125 | convolution fusion | flops 817889792 | bytes 16015360 | tf_op jit(solution)/shard_map/sub | solution.py:42
  214.0 9.0 %fusion.9 = f32[12,512,128]{1,2,0:T(8,128)} fusion(bf16[512,12,128]{0,2,1:T(8,128)(2,1)} %copy.142, f32[12,512,512]{1,2,0:T(8,128)} %get-tuple-element.25, f32[12,512]{1,0:T(8,128)S(1)} %get-tuple-element.24), kind=kOutput, calls=%fused_computation.19 | convolution fusion | flops 811597824 | bytes 17326080 | tf_op jit(solution)/shard_map/hij,ihd->jhd/dot_general | solution.py:73
  223.0 11.3 %fusion.3 = (f32[12,512]{1,0:T(8,128)S(1)}, f32[12,512,512]{2,1,0:T(8,128)}) fusion(f32[12,512,512]{1,2,0:T(8,128)} %get-tuple-element.25, f32[12,512]{1,0:T(8,128)S(1)} %get-tuple-element.24, bf16[512,12,128]{0,2,1:T(8,128)(2,1)S(1)} %copy-done.14, bf16[512,12,128]{2,1,0:T(8,128)(2,1)S(1)} %copy-done.12), kind=kOutput, calls=%fused_computation.5 | convolution fusion | flops 814737408 | bytes 28360704 | tf_op jit(solution)/shard_map/ihd,jhd->hij/dot_general | solution.py:76
  235.6 7.0 %fusion.5 = bf16[12,512,512]{1,2,0:T(8,128)(2,1)S(1)} fusion(f32[12,512,512]{2,1,0:T(8,128)} %get-tuple-element.27, f32[12,512]{1,0:T(8,128)S(1)} %get-tuple-element.26, f32[12,512,512]{1,2,0:T(8,128)S(1)} %bitcast.124, f32[12,512]{1,0:T(8,128)S(1)} %get-tuple-element.24), kind=kLoop, calls=%fused_computation.7 | loop fusion | flops 12582912 | bytes 31506432 | tf_op jit(solution)/shard_map/convert_element_type | solution.py:80
  251.1 8.2 %fusion.73 = (f32[12,512]{1,0:T(8,128)S(1)}, f32[12,512,512]{1,2,0:T(8,128)}) fusion(f32[12,512,512]{1,2,0:T(8,128)S(1)} %fusion.48, pred[512,512]{0,1:T(8,128)(4,1)S(1)} %iota_compare_fusion), kind=kOutput, calls=%fused_computation.123 | output fusion | flops 18874880 | bytes 25452544 | tf_op jit(solution)/shard_map/sub | solution.py:42
  259.3 7.3 %fusion.51 = bf16[512,12,128]{0,2,1:T(8,128)(2,1)} fusion(f32[12,512,512]{1,2,0:T(8,128)} %get-tuple-element.21, f32[12,512]{1,0:T(8,128)S(1)} %get-tuple-element.20, bf16[512,12,128]{2,1,0:T(8,128)(2,1)S(1)} %copy-done.11), kind=kOutput, calls=%fused_computation.93 | convolution fusion | flops 812384256 | bytes 15753216 | tf_op jit(solution)/shard_map/hij,jhd->ihd/dot_general | solution.py:54
  266.5 4.4 copy.119
  289.1 4.9 %add_convert_fusion = bf16[512,1536]{1,0:T(8,128)(2,1)S(1)} fusion(f32[512,1536]{1,0:T(8,128)} %copy.143, f32[512,1536]{1,0:T(8,128)} %copy.140, f32[512,1536]{1,0:T(8,128)} %copy.137, f32[1536]{0:T(1024)S(1)} %reduce, f32[1536]{0:T(1024)S(1)} %reduce.2, f32[1536]{0:T(1024)S(1)} %reduce.1), kind=kLoop, calls=%fused_computation.72 | loop fusion | flops 4718592 | bytes 11028480 | tf_op jit(solution)/shard_map/convert_element_type | solution.py:91
  301.3 6.5 %all-to-all-start.6 = ((bf16[8,64,1536]{2,1,0:T(8,128)(2,1)}), bf16[8,64,1536]{2,1,0:T(8,128)(2,1)S(1)}, u32[]{:S(2)}, u32[]{:S(2)}) async-start(bf16[8,64,1536]{2,1,0:T(8,128)(2,1)} %fusion.59), calls=%async_computation.6 | async-start | bytes 3145728 | tf_op jit(solution)/shard_map/all_to_all | solution.py:93
  315.5 28.6 %all-to-all-done.6 = bf16[8,64,1536]{2,1,0:T(8,128)(2,1)S(1)} async-done(((bf16[8,64,1536]{2,1,0:T(8,128)(2,1)}), bf16[8,64,1536]{2,1,0:T(8,128)(2,1)S(1)}, u32[]{:S(2)}, u32[]{:S(2)}) %all-to-all-start.6) | async-done | bytes 1572896 | tf_op jit(solution)/shard_map/all_to_all | solution.py:93
  349.1 4.5 %all-to-all-start.2 = ((bf16[64,8,1536]{2,0,1:T(8,128)(2,1)}), bf16[64,8,1536]{2,0,1:T(8,128)(2,1)}, u32[]{:S(2)}, u32[]{:S(2)}) async-start(bf16[64,8,1536]{2,0,1:T(8,128)(2,1)} %bitcast.125), calls=%async_computation.2 | async-start | bytes 3145728 | tf_op jit(solution)/shard_map/all_to_all | solution.py:49
  361.4 17.8 %all-to-all-done.2 = bf16[64,8,1536]{2,0,1:T(8,128)(2,1)} async-done(((bf16[64,8,1536]{2,0,1:T(8,128)(2,1)}), bf16[64,8,1536]{2,0,1:T(8,128)(2,1)}, u32[]{:S(2)}, u32[]{:S(2)}) %all-to-all-start.2) | async-done | bytes 1572896 | tf_op jit(solution)/shard_map/all_to_all | solution.py:49
  388.3 8.2 %fusion.74 = (f32[12,512]{1,0:T(8,128)S(1)}, f32[12,512,512]{1,2,0:T(8,128)}) fusion(f32[12,512,512]{1,2,0:T(8,128)S(1)} %fusion.44, pred[512,512]{0,1:T(8,128)(4,1)S(1)} %iota_compare_fusion), kind=kOutput, calls=%fused_computation.124 | output fusion | flops 18874880 | bytes 25452544 | tf_op jit(solution)/shard_map/sub | solution.py:42
  396.5 6.1 %fusion.54 = bf16[512,12,128]{0,2,1:T(8,128)(2,1)S(1)} fusion(f32[12,512,512]{1,2,0:T(8,128)} %get-tuple-element.23, f32[12,512]{1,0:T(8,128)S(1)} %get-tuple-element.22, bf16[512,12,128]{2,1,0:T(8,128)(2,1)S(1)} %get-tuple-element.9), kind=kOutput, calls=%fused_computation.94 | convolution fusion | flops 812384256 | bytes 15753216 | tf_op jit(solution)/shard_map/hij,jhd->ihd/dot_general | solution.py:54
  405.7 4.1 all_to_all.68
  409.7 4.5 %all-to-all-start.3 = ((bf16[8,64,1536]{2,1,0:T(8,128)(2,1)}), bf16[8,64,1536]{2,1,0:T(8,128)(2,1)S(1)}, u32[]{:S(2)}, u32[]{:S(2)}) async-start(bf16[8,64,1536]{2,1,0:T(8,128)(2,1)} %all_to_all.68), calls=%async_computation.3 | async-start | bytes 3145728 | tf_op jit(solution)/shard_map/all_to_all | solution.py:56
  417.5 20.6 %all-to-all-done.3 = bf16[8,64,1536]{2,1,0:T(8,128)(2,1)S(1)} async-done(((bf16[8,64,1536]{2,1,0:T(8,128)(2,1)}), bf16[8,64,1536]{2,1,0:T(8,128)(2,1)S(1)}, u32[]{:S(2)}, u32[]{:S(2)}) %all-to-all-start.3) | async-done | bytes 1572896 | tf_op jit(solution)/shard_map/all_to_all | solution.py:56
  (116 shorter events, 112.9 us)
Async XLA Ops:
  0.6 3.7 collective-permute-start.5
  4.3 36.4 %collective-permute-start.6 = (bf16[64,12288]{1,0:T(8,128)(2,1)S(1)}, bf16[64,12288]{1,0:T(8,128)(2,1)S(1)}, u32[]{:S(2)}, u32[]{:S(2)}) collective-permute-start(bf16[64,12288]{1,0:T(8,128)(2,1)S(1)} %collective-permute-done.5), channel_id=1, source_target_pairs={{0,16},{8,24},{16,0},{24,8},{32,48},{40,56},{48,32},{56,40},{64,80... | collective-permute-start | bytes 4718600 | tf_op jit(solution)/shard_map/ppermute | solution.py:14
  6.0 38.1 %collective-permute-start.1 = (bf16[64,12288]{1,0:T(8,128)(2,1)}, bf16[64,12288]{1,0:T(8,128)(2,1)}, u32[]{:S(2)}, u32[]{:S(2)}) collective-permute-start(bf16[64,12288]{1,0:T(8,128)(2,1)} %bitcast.116), channel_id=1, source_target_pairs={{0,8},{8,0},{16,24},{24,16},{32,40},{40,32},{48,56},{56,48},{64,72... | collective-permute-start | bytes 4718600 | tf_op jit(solution)/shard_map/ppermute | solution.py:14
  40.8 38.9 %collective-permute-start.7 = (bf16[64,12288]{1,0:T(8,128)(2,1)S(1)}, bf16[64,12288]{1,0:T(8,128)(2,1)}, u32[]{:S(2)}, u32[]{:S(2)}) collective-permute-start(bf16[64,12288]{1,0:T(8,128)(2,1)S(1)} %collective-permute-done.6), channel_id=1, source_target_pairs={{0,32},{8,40},{16,48},{24,56},{32,0},{40,8},{48,16},{56,24},{64,96... | collective-permute-start | bytes 4718600 | tf_op jit(solution)/shard_map/ppermute | solution.py:14
  44.1 68.0 %collective-permute-start.2 = (bf16[64,12288]{1,0:T(8,128)(2,1)}, bf16[64,12288]{1,0:T(8,128)(2,1)}, u32[]{:S(2)}, u32[]{:S(2)}) collective-permute-start(bf16[64,12288]{1,0:T(8,128)(2,1)} %collective-permute-done.1), channel_id=1, source_target_pairs={{0,16},{8,24},{16,0},{24,8},{32,48},{40,56},{48,32},{56,40},{64,80... | collective-permute-start | bytes 4718600 | tf_op jit(solution)/shard_map/ppermute | solution.py:14
  79.6 48.3 %collective-permute-start.8 = (bf16[64,12288]{1,0:T(8,128)(2,1)}, bf16[64,12288]{1,0:T(8,128)(2,1)S(1)}, u32[]{:S(2)}, u32[]{:S(2)}) collective-permute-start(bf16[64,12288]{1,0:T(8,128)(2,1)} %collective-permute-done.7), channel_id=1, source_target_pairs={{0,64},{8,72},{16,80},{24,88},{32,96},{40,104},{48,112},{56,120},{... | collective-permute-start | bytes 4718600 | tf_op jit(solution)/shard_map/ppermute | solution.py:14
  83.6 8.9 %copy-start.2 = (bf16[1,64,12288]{2,1,0:T(8,128)(2,1)S(1)}, bf16[1,64,12288]{2,1,0:T(8,128)(2,1)}, u32[]{:S(2)}) copy-start(bf16[1,64,12288]{2,1,0:T(8,128)(2,1)} %param.7) | copy-start | bytes 4718596
  85.2 48.2 %all-to-all-start.5 = ((bf16[64,8,1536]{2,0,1:T(8,128)(2,1)}), bf16[64,8,1536]{2,0,1:T(8,128)(2,1)}, u32[]{:S(2)}, u32[]{:S(2)}) async-start(bf16[64,8,1536]{2,0,1:T(8,128)(2,1)} %copy.132), calls=%async_computation.5 | async-start | bytes 3145728 | tf_op jit(solution)/shard_map/all_to_all | solution.py:65
  112.1 64.9 %collective-permute-start.3 = (bf16[64,12288]{1,0:T(8,128)(2,1)}, bf16[64,12288]{1,0:T(8,128)(2,1)}, u32[]{:S(2)}, u32[]{:S(2)}) collective-permute-start(bf16[64,12288]{1,0:T(8,128)(2,1)} %collective-permute-done.2), channel_id=1, source_target_pairs={{0,32},{8,40},{16,48},{24,56},{32,0},{40,8},{48,16},{56,24},{64,96... | collective-permute-start | bytes 4718600 | tf_op jit(solution)/shard_map/ppermute | solution.py:14
  127.9 10.2 %copy-start = (bf16[64,12288]{1,0:T(8,128)(2,1)}, bf16[64,12288]{1,0:T(8,128)(2,1)S(1)}, u32[]{:S(2)}) copy-start(bf16[64,12288]{1,0:T(8,128)(2,1)S(1)} %collective-permute-done.8) | copy-start | bytes 4718596
  133.4 22.9 %all-to-all-start = ((bf16[64,8,1536]{2,0,1:T(8,128)(2,1)}), bf16[64,8,1536]{2,0,1:T(8,128)(2,1)}, u32[]{:S(2)}, u32[]{:S(2)}) async-start(bf16[64,8,1536]{2,0,1:T(8,128)(2,1)} %fusion.36), calls=%async_computation | async-start | bytes 3145728 | tf_op jit(solution)/shard_map/all_to_all | solution.py:49
  138.1 22.4 %copy-start.15 = (f32[1,1536]{1,0:T(1,128)S(1)}, f32[1,1536]{1,0:T(1,128)}, u32[]{:S(2)}) copy-start(f32[1,1536]{1,0:T(1,128)} %param.11) | copy-start | bytes 18436
  138.1 22.4 %copy-start.16 = (f32[1,1536]{1,0:T(1,128)S(1)}, f32[1,1536]{1,0:T(1,128)}, u32[]{:S(2)}) copy-start(f32[1,1536]{1,0:T(1,128)} %param.12) | copy-start | bytes 18436
  138.1 22.4 %copy-start.17 = (f32[1,1536]{1,0:T(1,128)S(1)}, f32[1,1536]{1,0:T(1,128)}, u32[]{:S(2)}) copy-start(f32[1,1536]{1,0:T(1,128)} %param.13) | copy-start | bytes 18436
  156.4 25.5 %all-to-all-start.4 = ((bf16[64,8,1536]{2,0,1:T(8,128)(2,1)}), bf16[64,8,1536]{2,0,1:T(8,128)(2,1)S(1)}, u32[]{:S(2)}, u32[]{:S(2)}) async-start(bf16[64,8,1536]{2,0,1:T(8,128)(2,1)} %bitcast.112), calls=%async_computation.4 | async-start | bytes 3145728 | tf_op jit(solution)/shard_map/all_to_all | solution.py:64
  177.0 138.5 %collective-permute-start.4 = (bf16[64,12288]{1,0:T(8,128)(2,1)}, bf16[64,12288]{1,0:T(8,128)(2,1)}, u32[]{:S(2)}, u32[]{:S(2)}) collective-permute-start(bf16[64,12288]{1,0:T(8,128)(2,1)} %collective-permute-done.3), channel_id=1, source_target_pairs={{0,64},{8,72},{16,80},{24,88},{32,96},{40,104},{48,112},{56,120},{... | collective-permute-start | bytes 4718600 | tf_op jit(solution)/shard_map/ppermute | solution.py:14
  214.0 9.0 %copy-start.12 = (bf16[512,12,128]{2,1,0:T(8,128)(2,1)S(1)}, bf16[512,12,128]{2,1,0:T(8,128)(2,1)}, u32[]{:S(2)}) copy-start(bf16[512,12,128]{2,1,0:T(8,128)(2,1)} %get-tuple-element.19) | copy-start | bytes 4718596
  214.0 9.0 %copy-start.14 = (bf16[512,12,128]{0,2,1:T(8,128)(2,1)S(1)}, bf16[512,12,128]{0,2,1:T(8,128)(2,1)}, u32[]{:S(2)}) copy-start(bf16[512,12,128]{0,2,1:T(8,128)(2,1)} %copy.142) | copy-start | bytes 4718596
  223.0 11.3 %slice-start = ((s8[12582912]{0:T(1024)(128)(4,1)}), s8[4194304]{0:T(1024)(128)(4,1)S(1)}, s32[]{:S(2)}) async-start(s8[12582912]{0:T(1024)(128)(4,1)} %bitcast.123), calls=%async_computation.7 | async-start | bytes 8388608
  223.0 11.3 %slice-start.1 = ((s8[12582912]{0:T(1024)(128)(4,1)}), s8[4194304]{0:T(1024)(128)(4,1)S(1)}, s32[]{:S(2)}) async-start(s8[12582912]{0:T(1024)(128)(4,1)} %bitcast.123), calls=%async_computation.8 | async-start | bytes 8388608
  223.0 12.6 %slice-start.2 = ((s8[12582912]{0:T(1024)(128)(4,1)}), s8[4194304]{0:T(1024)(128)(4,1)S(1)}, s32[]{:S(2)}) async-start(s8[12582912]{0:T(1024)(128)(4,1)} %bitcast.123), calls=%async_computation.9 | async-start | bytes 8388608
  235.6 7.1 %copy-start.9 = (bf16[512,12,128]{0,2,1:T(8,128)(2,1)S(1)}, bf16[512,12,128]{0,2,1:T(8,128)(2,1)}, u32[]{:S(2)}) copy-start(bf16[512,12,128]{0,2,1:T(8,128)(2,1)} %copy.138) | copy-start | bytes 4718596
  246.5 2.7 copy-start.7
  246.5 2.7 copy-start.8
  251.0 8.2 %copy-start.11 = (bf16[512,12,128]{2,1,0:T(8,128)(2,1)S(1)}, bf16[512,12,128]{2,1,0:T(8,128)(2,1)}, u32[]{:S(2)}) copy-start(bf16[512,12,128]{2,1,0:T(8,128)(2,1)} %get-tuple-element.12) | copy-start | bytes 4718596
  274.9 25.3 %all-to-all-start.1 = ((bf16[8,64,1536]{2,1,0:T(8,128)(2,1)}), bf16[8,64,1536]{2,1,0:T(8,128)(2,1)S(1)}, u32[]{:S(2)}, u32[]{:S(2)}) async-start(bf16[8,64,1536]{2,1,0:T(8,128)(2,1)} %all_to_all.64), calls=%async_computation.1 | async-start | bytes 3145728 | tf_op jit(solution)/shard_map/all_to_all | solution.py:56
  301.3 42.8 %all-to-all-start.6 = ((bf16[8,64,1536]{2,1,0:T(8,128)(2,1)}), bf16[8,64,1536]{2,1,0:T(8,128)(2,1)S(1)}, u32[]{:S(2)}, u32[]{:S(2)}) async-start(bf16[8,64,1536]{2,1,0:T(8,128)(2,1)} %fusion.59), calls=%async_computation.6 | async-start | bytes 3145728 | tf_op jit(solution)/shard_map/all_to_all | solution.py:93
  313.1 33.6 %collective-permute-start = (bf16[64,12288]{1,0:T(8,128)(2,1)}, bf16[64,12288]{1,0:T(8,128)(2,1)}, u32[]{:S(2)}, u32[]{:S(2)}) collective-permute-start(bf16[64,12288]{1,0:T(8,128)(2,1)} %fusion.26), channel_id=1, source_target_pairs={{0,8},{8,16},{16,24},{24,32},{32,40},{40,48},{48,56},{56,64},{64,7... | collective-permute-start | bytes 4718600 | tf_op jit(solution)/shard_map/ppermute | solution.py:20
  349.1 30.1 %all-to-all-start.2 = ((bf16[64,8,1536]{2,0,1:T(8,128)(2,1)}), bf16[64,8,1536]{2,0,1:T(8,128)(2,1)}, u32[]{:S(2)}, u32[]{:S(2)}) async-start(bf16[64,8,1536]{2,0,1:T(8,128)(2,1)} %bitcast.125), calls=%async_computation.2 | async-start | bytes 3145728 | tf_op jit(solution)/shard_map/all_to_all | solution.py:49
  353.6 4.0 copy-start.6
  405.7 8.5 %copy-start.3 = (bf16[1,64,12288]{2,1,0:T(8,128)(2,1)S(1)}, bf16[1,64,12288]{2,1,0:T(8,128)(2,1)}, u32[]{:S(2)}) copy-start(bf16[1,64,12288]{2,1,0:T(8,128)(2,1)} %param.7) | copy-start | bytes 4718596
  409.7 28.3 %all-to-all-start.3 = ((bf16[8,64,1536]{2,1,0:T(8,128)(2,1)}), bf16[8,64,1536]{2,1,0:T(8,128)(2,1)S(1)}, u32[]{:S(2)}, u32[]{:S(2)}) async-start(bf16[8,64,1536]{2,1,0:T(8,128)(2,1)} %all_to_all.68), calls=%async_computation.3 | async-start | bytes 3145728 | tf_op jit(solution)/shard_map/all_to_all | solution.py:56
  (5 other events, 7.4 us)
